TPU v7x, 256 devices: a whole 4x4x8 slice. The times are simulated.
256 devices in a mesh: dp: 32 (over x_lo, z, core), expert: 8 (over x_hi, y).
Axes of the slice: x: 4 (x_hi: 2, x_lo: 2; x = x_hi * 2 + x_lo), y: 4, z: 8, core: 2. Of those that a mesh axis runs over, the one named last changes fastest.
Arguments:
- tokens: bfloat16 [49152, 4096], P(('dp', 'expert')), may hold values from -24 to 24
- routes: int32 [49152, 2], P(('dp', 'expert')), may hold values from 0 to 7, all different within a row; in each aligned block of 192 rows (0 to 191, 192 to 383, ...) at most 64 rows name the same one
- positives: int32 [512], P(('dp', 'expert')), may hold values from 0 to 511, each once
- expert_out: bfloat16 [32, 8, 8, 64, 4096], P('dp', 'expert'), may hold values from -6 to 6
- router: bfloat16 [4096, 8], replicated, may hold values from -0.09375 to 0.09375
- norm_gain: float32 [4096], replicated, may hold values from 0.25 to 1.75
- loss_scale: float32 [], replicated, may hold values from 8192 to 65536
Outputs:
- token_grad: bfloat16 [49152, 4096], P(('dp', 'expert'))
- expert_grad: bfloat16 [32, 8, 8, 64, 4096], P('dp', 'expert')
- router_grad: float32 [4096, 8], replicated
- loss: float32 [], replicated
Inputs may be any that keep to these rules, and one draw needn't show every extreme that they name: `routes`: each row names 2 different experts; among the rows of one device no expert is named by more than 64 rows, a bound that some block reaches. `positives`: A permutation of the records.
All inputs are finite; a program needn't handle non-finite values.
Results may differ from a plain program's by a relative error of at most 0.0061.
Values may be sent and summed in bfloat16 or wider, within the bound.
No kernel may reach another device: no remote copies, remote signals or barrier semaphores. Data moves between devices by JAX's collectives and lax.ppermute only.
A program may use at most 128 MiB of HBM per device.

v0:
```python
import math
import jax
import jax.numpy as jnp
from jax import lax
from jax.sharding import PartitionSpec as P

PAIR_DEV = 2
SEQ = 48
norm_eps = 1e-05


def slot_where(routes, experts, capacity):
    hit_table = (routes[:, :, None] == jnp.arange(experts, dtype=jnp.int32)[None, None, :]).astype(
        jnp.int32
    )
    flat_hits = hit_table.reshape(-1, experts)
    before = jnp.cumsum(flat_hits, axis=0) - flat_hits
    slot_rank = jnp.sum(before * flat_hits, axis=1).reshape(routes.shape)
    return routes * capacity + slot_rank


def forward_rows(tokens, routes, received, router, norm_gain):
    experts = received.shape[0]
    capacity = received.shape[1]
    hidden_width = received.shape[2]
    logits = jnp.dot(tokens, router, preferred_element_type=jnp.float32)
    one_hot = (routes[:, :, None] == jnp.arange(experts, dtype=jnp.int32)[None, None, :]).astype(
        jnp.float32
    )
    chosen = jnp.sum(one_hot * logits[:, None, :], axis=2)
    gate_mix = jax.nn.softmax(chosen, axis=1)
    slot_rows = slot_where(routes, experts, capacity)
    fetched = received.reshape(experts * capacity, hidden_width)[slot_rows]
    summed_rows = (
        tokens.astype(jnp.float32)
        + gate_mix[:, 0:1] * fetched[:, 0].astype(jnp.float32)
        + gate_mix[:, 1:2] * fetched[:, 1].astype(jnp.float32)
    )
    inverse = lax.rsqrt(jnp.mean(summed_rows * summed_rows, axis=1, keepdims=True) + norm_eps)
    normed = summed_rows * inverse * norm_gain
    pooled = jnp.mean(normed.reshape(-1, SEQ, hidden_width), axis=1).astype(jnp.bfloat16)
    return (pooled, (gate_mix, one_hot, slot_rows, fetched, summed_rows, inverse))


def backward_rows(tokens, router, norm_gain, saved, grad_pool, experts, capacity):
    gate_mix, one_hot, slot_rows, fetched, summed_rows, inverse = saved
    hidden_width = tokens.shape[1]
    grad_rows = jnp.broadcast_to(
        grad_pool[:, None, :] / SEQ, (grad_pool.shape[0], SEQ, hidden_width)
    ).reshape(-1, hidden_width)
    weighted = grad_rows * norm_gain
    grad_summed = inverse * weighted - summed_rows * inverse**3 * jnp.mean(
        weighted * summed_rows, axis=1, keepdims=True
    )
    grad_gate = jnp.sum(grad_summed[:, None, :] * fetched.astype(jnp.float32), axis=2)
    grad_chosen = gate_mix * (grad_gate - jnp.sum(gate_mix * grad_gate, axis=1, keepdims=True))
    grad_logits = jnp.sum(one_hot * grad_chosen[:, :, None], axis=1).astype(jnp.bfloat16)
    router_part = lax.dot_general(
        tokens, grad_logits, (((0,), (0,)), ((), ())), preferred_element_type=jnp.float32
    )
    through_router = lax.dot_general(
        grad_logits, router, (((1,), (1,)), ((), ())), preferred_element_type=jnp.float32
    )
    token_grad = (grad_summed + through_router).astype(jnp.bfloat16)
    outgoing = (
        (gate_mix[:, :, None] * grad_summed[:, None, :])
        .astype(jnp.bfloat16)
        .reshape(-1, hidden_width)
    )
    sendback = (
        jnp.zeros((experts * capacity, hidden_width), jnp.bfloat16)
        .at[slot_rows.reshape(-1)]
        .set(outgoing)
    )
    return (token_grad, sendback.reshape(experts, capacity, hidden_width), router_part)


def score_rows(queries, records_all, positives, loss_scale, pair_total, score_scale):
    scores = (
        lax.dot_general(
            queries, records_all, (((1,), (1,)), ((), ())), preferred_element_type=jnp.float32
        )
        * score_scale
    )
    highest = jnp.max(scores, axis=1, keepdims=True)
    log_total = highest[:, 0] + jnp.log(jnp.sum(jnp.exp(scores - highest), axis=1))
    is_positive = jnp.arange(pair_total, dtype=jnp.int32)[None, :] == positives[:, None]
    positive_score = jnp.sum(jnp.where(is_positive, scores, jnp.zeros_like(scores)), axis=1)
    row_loss = log_total - positive_score
    softmax_rows = jnp.exp(scores - log_total[:, None])
    score_grad = (
        (softmax_rows - is_positive.astype(jnp.float32)) * (loss_scale / pair_total)
    ).astype(jnp.bfloat16)
    return (row_loss, score_grad)


def shards(tokens, routes, positives, expert_out, router, norm_gain, loss_scale):
    experts = expert_out.shape[2]
    capacity = expert_out.shape[3]
    hidden_width = expert_out.shape[4]
    received = lax.all_to_all(
        expert_out.reshape(experts, capacity, hidden_width),
        "expert",
        split_axis=0,
        concat_axis=0,
        tiled=True,
    )
    pooled, saved = forward_rows(tokens, routes, received, router, norm_gain)
    queries = pooled[:PAIR_DEV]
    records = pooled[PAIR_DEV:]
    loop_size = lax.axis_size("dp")
    column_size = lax.axis_size("expert")
    device_count = loop_size * column_size
    pair_total = PAIR_DEV * device_count
    score_scale = 4.0 / math.sqrt(hidden_width)
    records_all = lax.all_gather(records, ("dp", "expert"), axis=0, tiled=True)
    row_loss, score_grad = score_rows(
        queries, records_all, positives, loss_scale, pair_total, score_scale
    )
    loss_local = jnp.sum(row_loss)
    grad_queries = (
        jnp.dot(score_grad, records_all, preferred_element_type=jnp.float32) * score_scale
    )
    grad_records = lax.psum_scatter(
        lax.dot_general(
            score_grad, queries, (((0,), (0,)), ((), ())), preferred_element_type=jnp.float32
        )
        * score_scale,
        ("dp", "expert"),
        scatter_dimension=0,
        tiled=True,
    )
    grad_pool = jnp.concatenate([grad_queries, grad_records], axis=0)
    token_grad, sendback, router_part = backward_rows(
        tokens, router, norm_gain, saved, grad_pool, experts, capacity
    )
    returned = lax.all_to_all(sendback, "expert", split_axis=0, concat_axis=0, tiled=True)
    router_grad, loss_total = lax.psum((router_part, loss_local), ("dp", "expert"))
    expert_grad = returned.reshape(1, 1, experts, capacity, hidden_width)
    return (token_grad, expert_grad, router_grad, loss_total / pair_total)


def solution(mesh):
    placed = (
        P(("dp", "expert"), None),
        P(("dp", "expert"), None),
        P(("dp", "expert")),
        P("dp", "expert", None, None, None),
        P(),
        P(),
        P(),
    )
    return jax.shard_map(
        shards,
        mesh=mesh,
        in_specs=placed,
        out_specs=(P(("dp", "expert"), None), P("dp", "expert", None, None, None), P(), P()),
        check_vma=False,
    )
```

profile of v0, /device:TPU:8, one launch (start us, length us, event | category | flops | bytes accessed | tf_op | source)
XLA Modules:
  0.0 1506.5 jit_solution(1943185011051784695)
XLA Ops:
  7.2 0.0 copy-start
  7.2 0.0 copy-start.8
  7.2 0.0 copy-start.4
  7.2 7.5 all-to-all-start
  14.7 0.0 all-gather.3.cloned.1.call-start
  14.7 0.1 copy.45
  14.9 0.1 eq.59
  15.0 0.1 eq.55
  15.2 0.9 reduce-window.6
  16.0 0.2 slice_reduce_fusion
  16.3 0.1 fusion.7
  16.4 0.1 reshape.211
  16.5 0.1 copy.47
  16.6 0.1 copy.48
  16.8 0.1 reshape.221
  16.9 0.0 copy-done
  16.9 0.0 copy-done.4
  16.9 0.5 fusion.20
  17.5 45.7 %all-to-all-done = bf16[8,64,4096]{2,1,0:T(8,128)(2,1)} async-done(((bf16[8,64,4096]{2,1,0:T(8,128)(2,1)}), bf16[8,64,4096]{2,1,0:T(8,128)(2,1)}, u32[]{:S(2)}, u32[]{:S(2)}) %all-to-all-start) | async-done | bytes 4194336 | tf_op jit(solution)/shard_map/all_to_all | solution.py:101
  63.2 11.0 gather_fusion
  74.2 4.6 reshape.220
  78.8 0.0 copy-start.5
  78.8 7.0 fusion.17
  85.8 0.0 copy-start.6
  85.8 4.0 multiply_reduce_fusion.2
  89.9 2.4 multiply_multiply_fusion
  92.3 0.2 copy-done.2
  92.5 2.2 reduce_sum.112
  94.7 0.6 slice_bitcast_fusion
  95.3 0.0 all-gather.3.cloned.1.call-update
  95.3 0.2 all-reduce.6.cloned.1.call-start
  96.2 680.8 %all-gather.3.cloned.1.call-done = bf16[256,2,4096]{2,1,0:T(2,128)(2,1)} async-done(((bf16[1,2,4096]{2,1,0:T(2,128)(2,1)}), bf16[256,2,4096]{2,1,0:T(2,128)(2,1)}) %all-gather.3.cloned.1.call-update) | async-done | bytes 4194320 | tf_op jit(solution)/shard_map/all_gather | solution.py:116
  777.0 7.2 reshape.238
  784.2 3.5 fusion.19
  787.7 0.2 select_reduce_fusion.2
  787.9 0.6 subtract_reduce_fusion
  788.5 4.6 convolution_multiply_fusion
  793.1 0.0 all-reduce.6.cloned.1.call-update
  793.1 0.1 copy.54
  793.3 0.1 div.48
  793.4 0.1 copy.53
  793.5 0.1 reshape.214
  793.7 2.9 convolution_multiply_fusion.1
  796.6 301.1 %all-reduce.6.cloned.1.call-done = f32[512,4096]{1,0:T(8,128)} async-done(((f32[512,4096]{1,0:T(8,128)}), f32[512,4096]{1,0:T(8,128)}) %all-reduce.6.cloned.1.call-update) | async-done | bytes 8388624
  1097.7 1.1 constant_dynamic-slice_fusion
  1098.8 0.3 bitcast_multiply_fusion
  1099.2 0.5 copy-done.3
  1099.7 0.4 multiply_reduce_fusion.1
  1100.1 0.7 multiply_subtract_fusion
  1100.8 1.7 copy-done.1
  1102.5 5.3 mul.182
  1107.8 8.4 mul.189
  1116.2 9.7 scatter_custom_fusion
  1125.9 6.8 all-to-all-start.1
  1132.6 112.4 %psum.15 = f32[]{:T(128)} all-reduce(f32[]{:T(128)} %get-tuple-element.6), channel_id=1, replica_groups=mesh['dp'=32,'expert'=8] {'dp','expert'}, use_global_device_ids=true, to_apply=%region_19.20 | all-reduce | flops 1 | bytes 8 | tf_op jit(solution)/shard_map/psum | solution.py:138
  1245.7 5.7 multiply_reduce_fusion
  1251.4 0.1 copy.52
  1251.5 2.4 convolution_bitcast_fusion
  1253.9 0.0 all-reduce.4.cloned.1.call-update
  1254.0 3.6 fusion
  1257.6 0.0 all-to-all-done.1
  1257.6 235.8 %all-reduce.4.cloned.1.call-done = f32[4096,8]{0,1:T(8,128)} async-done(((f32[4096,8]{0,1:T(8,128)}), f32[4096,8]{0,1:T(8,128)}) %all-reduce.4.cloned.1.call-update) | async-done | bytes 131088 | tf_op jit(solution)/shard_map/psum | solution.py:138
  1493.4 4.7 copy.69
  1498.2 0.7 copy.70
  (28 shorter events, 0.3 us)
Async XLA Ops:
  7.2 9.7 copy-start
  7.2 7.5 copy-start.8
  7.2 9.7 copy-start.4
  7.2 56.0 %all-to-all-start = ((bf16[8,64,4096]{2,1,0:T(8,128)(2,1)}), bf16[8,64,4096]{2,1,0:T(8,128)(2,1)}, u32[]{:S(2)}, u32[]{:S(2)}) async-start(bf16[8,64,4096]{2,1,0:T(8,128)(2,1)} %bitcast.46), calls=%async_computation | async-start | bytes 8388608 | tf_op jit(solution)/shard_map/all_to_all | solution.py:101
  14.7 762.3 %all-gather.3.cloned.1.call-start = ((), (), s32[]{:S(2)}) async-start(), calls=%async_computation.3 | async-start | bytes 4210688 | tf_op jit(solution)/shard_map/all_gather | solution.py:116
  78.8 7.0 copy-start.5
  85.8 4.1 copy-start.6
  89.8 2.6 copy-start.2
  95.3 1002.4 %all-reduce.6.cloned.1.call-start = ((), (), s32[]{:S(2)}) async-start(), calls=%async_computation.4 | async-start | bytes 16777216
  784.2 3.5 copy-start.9
  1097.7 2.0 copy-start.3
  1100.8 1.7 copy-start.1
  1125.9 131.7 %all-to-all-start.1 = ((bf16[8,64,4096]{2,1,0:T(8,128)(2,1)}), bf16[8,64,4096]{2,1,0:T(8,128)(2,1)}, u32[]{:S(2)}, u32[]{:S(2)}) async-start(bf16[8,64,4096]{2,1,0:T(8,128)(2,1)} %bitcast.44), calls=%async_computation.1 | async-start | bytes 8388608 | tf_op jit(solution)/shard_map/all_to_all | solution.py:137
  1132.6 360.8 %all-reduce.4.cloned.1.call-start = ((), (), s32[]{:S(2)}) async-start(), calls=%async_computation.2 | async-start | bytes 262144 | tf_op jit(solution)/shard_map/psum | solution.py:138
  1493.4 4.7 copy-start.7
Sparse Core Ops, SparseCore 0:
  95.4 681.5 all-gather.2
  793.3 304.4 all-reduce.5
  1254.1 239.3 all-reduce.3
where the time goes:
time: 1510 us
  waiting for transfers between devices  1260 us (83%)
  blocking collectives  112 us (7%)
  local copies, waits for them, and re-layouts  54.7 us (4%)
  other arithmetic  27.5 us (2%)
  matrix products  17.5 us (1%)
  between operations  16.5 us (1%)
    all_gather x1, waiting for transfers between devices, shards(): records_all = lax.all_gather(records, ('dp', 'expert'), axis=0, tiled=True)  681 us
    unnamed x4, waiting for transfers between devices  301 us
    psum x1, waiting for transfers between devices, shards(): lax.psum((router_part, loss_local), ('dp', 'expert'))  236 us
    psum x1, blocking collectives, shards(): lax.psum((router_part, loss_local), ('dp', 'expert'))  112 us
    all_to_all x1, waiting for transfers between devices, shards(): lax.all_to_all(expert_out.reshape(experts, capacity, hidden_width), 'expe...  45.7 us
  transfers between devices with their start and end apart: 5, of which 4 were waited for; matrix products, arithmetic and copies ran while one was open for 1% of the time, Pallas kernels for 0%

commit v1 on v0

--- a/solution.py
+++ b/solution.py
@@ -135,7 +135,7 @@
         tokens, router, norm_gain, saved, grad_pool, experts, capacity
     )
     returned = lax.all_to_all(sendback, "expert", split_axis=0, concat_axis=0, tiled=True)
-    router_grad, loss_total = lax.psum((router_part, loss_local), ("dp", "expert"))
+    router_grad, loss_total = lax.psum(lax.psum((router_part, loss_local), "expert"), "dp")
     expert_grad = returned.reshape(1, 1, experts, capacity, hidden_width)
     return (token_grad, expert_grad, router_grad, loss_total / pair_total)
 

time: 1510 us -> 1460 us (0.967)
  waiting for transfers between devices: 1260 us -> 1220 us
    psum x1 -> x2, waiting for transfers between devices: 236 us -> 191 us  [the longest x1 191 us: shards(): lax.psum(lax.psum((router_part, loss_local), 'expert'), 'dp')]
    psum x1 -> x2, blocking collectives: 112 us -> 107 us  [the longest x1 53.9 us: shards(): lax.psum(lax.psum((router_part, loss_local), 'expert'), 'dp')]
    unnamed x4 -> x5, waiting for transfers between devices: 301 us -> 301 us
  transfers between devices with their start and end apart: 5 -> 6, of which waited for: 4 -> 4; matrix products, arithmetic and copies ran while one was open for 1% -> 1% of each run, Pallas kernels for 0% -> 0%
where the time goes in v1:
time: 1460 us
  waiting for transfers between devices  1220 us (84%)
  blocking collectives  107 us (7%)
  local copies, waits for them, and re-layouts  54.7 us (4%)
  other arithmetic  27.5 us (2%)
  matrix products  17.5 us (1%)
  between operations  16.5 us (1%)
  starting transfers between devices  14.6 us (1%)
    all_gather x1, waiting for transfers between devices, shards(): records_all = lax.all_gather(records, ('dp', 'expert'), axis=0, tiled=True)  681 us
    unnamed x5, waiting for transfers between devices  301 us
    psum x1, waiting for transfers between devices, shards(): lax.psum(lax.psum((router_part, loss_local), 'expert'), 'dp')  191 us
    psum x1, blocking collectives, shards(): lax.psum(lax.psum((router_part, loss_local), 'expert'), 'dp')  53.9 us
    psum x1, blocking collectives, shards(): lax.psum((router_part, loss_local), 'expert')  53.6 us
    all_to_all x1, waiting for transfers between devices, shards(): lax.all_to_all(expert_out.reshape(experts, capacity, hidden_width), 'expe...  45.7 us
  transfers between devices with their start and end apart: 6, of which 4 were waited for; matrix products, arithmetic and copies ran while one was open for 1% of the time, Pallas kernels for 0%

profile of v1, /device:TPU:8, one launch (start us, length us, event | category | flops | bytes accessed | tf_op | source)
XLA Modules:
  0.0 1457.3 jit_solution(15537055974868488303)
XLA Ops:
  7.2 0.0 copy-start
  7.2 0.0 copy-start.4
  7.2 7.5 all-to-all-start
  14.7 0.1 copy.45
  14.9 0.1 eq.59
  15.0 0.1 eq.55
  15.2 0.9 reduce-window.6
  16.0 0.2 slice_reduce_fusion
  16.3 0.1 fusion.7
  16.4 0.1 reshape.211
  16.5 0.1 copy.47
  16.6 0.1 copy.48
  16.7 0.1 reshape.221
  16.9 0.5 fusion.20
  17.5 45.7 %all-to-all-done = bf16[8,64,4096]{2,1,0:T(8,128)(2,1)} async-done(((bf16[8,64,4096]{2,1,0:T(8,128)(2,1)}), bf16[8,64,4096]{2,1,0:T(8,128)(2,1)}, u32[]{:S(2)}, u32[]{:S(2)}) %all-to-all-start) | async-done | bytes 4194336 | tf_op jit(solution)/shard_map/all_to_all | solution.py:101
  63.2 11.0 gather_fusion
  74.2 4.6 reshape.220
  78.8 0.0 copy-start.5
  78.8 7.0 fusion.17
  85.8 0.0 copy-start.6
  85.8 4.0 multiply_reduce_fusion.2
  89.9 2.4 multiply_multiply_fusion
  92.3 0.2 copy-done.2
  92.5 2.2 reduce_sum.112
  94.7 0.6 slice_bitcast_fusion
  95.3 0.0 all-gather.3.cloned.1.call-update
  95.3 0.2 all-reduce.9.cloned.1.call-start
  96.2 680.8 %all-gather.3.cloned.1.call-done = bf16[256,2,4096]{2,1,0:T(2,128)(2,1)} async-done(((bf16[1,2,4096]{2,1,0:T(2,128)(2,1)}), bf16[256,2,4096]{2,1,0:T(2,128)(2,1)}) %all-gather.3.cloned.1.call-update) | async-done | bytes 4194320 | tf_op jit(solution)/shard_map/all_gather | solution.py:116
  777.0 7.2 reshape.238
  784.2 3.5 fusion.19
  787.7 0.2 select_reduce_fusion.2
  787.9 0.6 subtract_reduce_fusion
  788.5 4.6 convolution_multiply_fusion
  793.1 0.0 all-reduce.9.cloned.1.call-update
  793.1 0.1 copy.54
  793.3 0.1 div.48
  793.4 0.1 copy.53
  793.5 0.1 reshape.214
  793.7 2.9 convolution_multiply_fusion.1
  796.6 301.1 %all-reduce.9.cloned.1.call-done = f32[512,4096]{1,0:T(8,128)} async-done(((f32[512,4096]{1,0:T(8,128)}), f32[512,4096]{1,0:T(8,128)}) %all-reduce.9.cloned.1.call-update) | async-done | bytes 8388624
  1097.7 1.1 constant_dynamic-slice_fusion
  1098.8 0.3 bitcast_multiply_fusion
  1099.2 0.5 copy-done.3
  1099.7 0.4 multiply_reduce_fusion.1
  1100.1 0.7 multiply_subtract_fusion
  1100.8 1.7 copy-done.1
  1102.5 5.3 mul.182
  1107.8 8.4 mul.189
  1116.2 9.7 scatter_custom_fusion
  1125.9 6.8 all-to-all-start.1
  1132.6 5.7 multiply_reduce_fusion
  1138.4 0.1 copy.52
  1138.5 2.4 convolution_bitcast_fusion
  1140.9 0.0 all-reduce.5.cloned.1.call-update
  1140.9 0.0 all-reduce.7.cloned.1.call-start
  1141.0 53.6 %psum.30 = f32[]{:T(128)} all-reduce(f32[]{:T(128)} %get-tuple-element.6), channel_id=1, replica_groups=mesh['dp'=32,'expert'=8] {'expert'}, use_global_device_ids=true, to_apply=%region_20.21 | all-reduce | flops 1 | bytes 8 | tf_op jit(solution)/shard_map/psum | solution.py:138
  1194.5 53.9 %psum.31 = f32[]{:T(128)} all-reduce(f32[]{:T(128)} %psum.30), channel_id=1, replica_groups=mesh['dp'=32,'expert'=8] {'dp'}, use_global_device_ids=true, to_apply=%region_21.22 | all-reduce | flops 1 | bytes 8 | tf_op jit(solution)/shard_map/psum | solution.py:138
  1249.1 0.0 all-reduce.5.cloned.1.call-done
  1249.1 0.0 all-reduce.7.cloned.1.call-update
  1249.1 3.6 fusion
  1252.8 0.0 all-to-all-done.1
  1252.8 191.4 %all-reduce.7.cloned.1.call-done = f32[4096,8]{0,1:T(8,128)} async-done(((f32[4096,8]{0,1:T(8,128)}), f32[4096,8]{0,1:T(8,128)}) %all-reduce.7.cloned.1.call-update) | async-done | bytes 131088 | tf_op jit(solution)/shard_map/psum | solution.py:138
  1444.2 4.7 copy.70
  1449.0 0.7 copy.71
  (32 shorter events, 0.3 us)
Async XLA Ops:
  7.2 9.7 copy-start
  7.2 7.5 copy-start.8
  7.2 9.7 copy-start.4
  7.2 56.0 %all-to-all-start = ((bf16[8,64,4096]{2,1,0:T(8,128)(2,1)}), bf16[8,64,4096]{2,1,0:T(8,128)(2,1)}, u32[]{:S(2)}, u32[]{:S(2)}) async-start(bf16[8,64,4096]{2,1,0:T(8,128)(2,1)} %bitcast.46), calls=%async_computation | async-start | bytes 8388608 | tf_op jit(solution)/shard_map/all_to_all | solution.py:101
  14.7 762.3 %all-gather.3.cloned.1.call-start = ((), (), s32[]{:S(2)}) async-start(), calls=%async_computation.4 | async-start | bytes 4210688 | tf_op jit(solution)/shard_map/all_gather | solution.py:116
  78.8 7.0 copy-start.5
  85.8 4.1 copy-start.6
  89.8 2.6 copy-start.2
  95.3 1002.4 %all-reduce.9.cloned.1.call-start = ((), (), s32[]{:S(2)}) async-start(), calls=%async_computation.5 | async-start | bytes 16777216
  784.2 3.5 copy-start.9
  1097.7 2.0 copy-start.3
  1100.8 1.7 copy-start.1
  1125.9 126.9 %all-to-all-start.1 = ((bf16[8,64,4096]{2,1,0:T(8,128)(2,1)}), bf16[8,64,4096]{2,1,0:T(8,128)(2,1)}, u32[]{:S(2)}, u32[]{:S(2)}) async-start(bf16[8,64,4096]{2,1,0:T(8,128)(2,1)} %bitcast.44), calls=%async_computation.1 | async-start | bytes 8388608 | tf_op jit(solution)/shard_map/all_to_all | solution.py:137
  1132.6 116.4 %all-reduce.5.cloned.1.call-start = ((), (), s32[]{:S(2)}) async-start(), calls=%async_computation.2 | async-start | bytes 262144 | tf_op jit(solution)/shard_map/psum | solution.py:138
  1140.9 303.3 %all-reduce.7.cloned.1.call-start = ((), (), s32[]{:S(2)}) async-start(), calls=%async_computation.3 | async-start | bytes 262144 | tf_op jit(solution)/shard_map/psum | solution.py:138
  1444.2 4.7 copy-start.7
Sparse Core Ops, SparseCore 0:
  95.4 681.5 all-gather.2
  793.3 304.4 all-reduce.8
  1141.0 96.2 all-reduce.4
  1249.2 194.9 all-reduce.6
